TPU v7x, 512 devices: a whole 4x4x16 slice. The times are simulated.
512 devices in a mesh: space: 128 (over z, y, core), tm: 4 (over x).
Axes of the slice: x: 4, y: 4, z: 16, core: 2. Of those that a mesh axis runs over, the one named last changes fastest.
Arguments:
- snapshots: bfloat16 [262144, 2048], P('space', 'tm'), as said below
- sketch: bfloat16 [2048, 256], P('tm'), may hold values from -0.125 to 0.125
- rotation: float32 [256, 256], replicated, may hold values from -0.375 to 0.375
Outputs:
- basis: float32 [262144, 256], P(('space', 'tm'))
- triangle: float32 [256, 256], replicated
Inputs may be any that keep to these rules, and one draw needn't show every extreme that they name: `snapshots`: the sketch has full column rank.
All inputs are finite; a program needn't handle non-finite values.
Results may differ from a plain program's by a relative error of at most 0.0003.
Values sent between devices are 32-bit elements; how exact they have to be, the bound alone decides.
A program may use at most 64 MiB of HBM per device.

v0:
```python
import jax
import jax.numpy as jnp
from jax import lax
from jax.sharding import PartitionSpec as P


def shards(snapshots, sketch, rotation):
    sketched = lax.psum_scatter(
        jnp.dot(snapshots, sketch, preferred_element_type=jnp.float32),
        "tm",
        scatter_dimension=0,
        tiled=True,
    )
    gram = lax.dot_general(
        sketched,
        sketched,
        (((0,), (0,)), ((), ())),
        precision=lax.Precision.HIGHEST,
        preferred_element_type=jnp.float32,
    )
    gram = lax.psum(gram, ("space", "tm"))
    lower = jnp.linalg.cholesky(gram)
    orthonormal = lax.linalg.triangular_solve(
        lower, sketched, left_side=False, lower=True, transpose_a=True
    )
    cell_count = sketched.shape[0] * lax.axis_size("space") * lax.axis_size("tm")
    scale = jnp.sqrt(jnp.float32(cell_count))
    basis = scale * jnp.dot(
        orthonormal, rotation, precision=lax.Precision.HIGHEST, preferred_element_type=jnp.float32
    )
    triangle = lower.T / scale
    return (basis, triangle)


def solution(mesh):
    in_specs = (P("space", "tm"), P("tm", None), P())
    out_specs = (P(("space", "tm"), None), P())
    return jax.shard_map(shards, mesh=mesh, in_specs=in_specs, out_specs=out_specs, check_vma=False)
```

profile of v0, /device:TPU:4, one launch (start us, length us, event | category | flops | bytes accessed | tf_op | source)
XLA Modules:
  0.0 592.6 jit_solution(8189028408867632442)
XLA Ops:
  7.2 0.0 copy-start
  7.2 0.0 reduce-scatter.2.cloned.1.call-start
  7.2 1.5 copy-done
  8.8 3.0 fusion.14
  11.8 0.0 reduce-scatter.2.cloned.1.call-update
  11.8 0.0 all-reduce.3.cloned.1.call-start
  11.8 40.3 %reduce-scatter.2.cloned.1.call-done = f32[512,256]{1,0:T(8,128)} async-done(((f32[2048,256]{1,0:T(8,128)}), f32[512,256]{1,0:T(8,128)}) %reduce-scatter.2.cloned.1.call-update) | async-done | bytes 524304 | tf_op jit(solution)/shard_map/reduce_scatter | solution.py:8
  52.2 2.9 fusion.15
  55.1 0.0 all-reduce.3.cloned.1.call-update
  55.1 0.0 copy-start.1
  55.1 462.1 %all-reduce.3.cloned.1.call-done = f32[256,256]{0,1:T(8,128)} async-done(((f32[256,256]{0,1:T(8,128)}), f32[256,256]{0,1:T(8,128)}) %all-reduce.3.cloned.1.call-update) | async-done | bytes 262160 | tf_op jit(solution)/shard_map/psum | solution.py:21
  517.2 1.1 copy.6
  518.3 1.0 fusion.5
  519.3 11.7 %cholesky.50 = f32[128,128]{1,0:T(8,128)S(1)} custom-call(f32[128,128]{1,0:T(8,128)S(1)} %cholesky.118), custom_call_target="Cholesky" | custom-call | tf_op jit(solution)/shard_map/jit(cholesky)/cholesky | solution.py:22
  531.1 9.8 %custom-call.14 = f32[1,128,128]{1,2,0:T(8,128)S(1)} custom-call(f32[1,128,128]{2,1,0:T(8,128)S(1)} %get-tuple-element.27), custom_call_target="InvertDiagBlocksLowerTriangular" | custom-call | tf_op jit(solution)/shard_map/jit(cholesky)/cholesky | solution.py:22
  540.9 0.2 constant_dynamic-update-slice_fusion.1
  541.1 0.3 convolution_subtract_fusion.1
  541.4 11.7 %cholesky.105 = f32[128,128]{1,0:T(8,128)S(1)} custom-call(f32[128,128]{1,0:T(8,128)S(1)} %convolution_subtract_fusion.1), custom_call_target="Cholesky" | custom-call | tf_op jit(solution)/shard_map/jit(cholesky)/cholesky | solution.py:22
  553.2 0.7 compare_reduce_fusion
  555.3 0.1 triangular_solve.58
  555.3 4.2 while.1
  555.5 0.6 fusion.26
  556.1 1.4 bitcast_dynamic-update-slice_fusion.2
  557.6 0.6 fusion.26
  558.1 1.4 bitcast_dynamic-update-slice_fusion.2
  559.6 0.0 copy-start.2
  559.6 0.6 copy-done.2
  560.2 20.5 %custom-call.15 = f32[2,128,128]{1,2,0:T(8,128)S(1)} custom-call(f32[2,128,128]{2,1,0:T(8,128)} %copy-done.2), custom_call_target="InvertDiagBlocksLowerTriangular" | custom-call | tf_op jit(solution)/shard_map/triangular_solve | solution.py:23
  580.7 0.0 copy-done.1
  580.7 0.4 fusion.3
  581.2 0.6 convolution_subtract_fusion
  581.8 0.4 fusion.7
  582.2 0.8 copy.7
  583.0 2.7 convolution_multiply_fusion
  (9 shorter events, 0.2 us)
Async XLA Ops:
  7.2 1.6 copy-start
  7.2 45.0 %reduce-scatter.2.cloned.1.call-start = ((), (), s32[]{:S(2)}) async-start(), calls=%async_computation.1 | async-start | bytes 2621440 | tf_op jit(solution)/shard_map/reduce_scatter | solution.py:8
  11.8 505.5 %all-reduce.3.cloned.1.call-start = ((), (), s32[]{:S(2)}) async-start(), calls=%async_computation.2 | async-start | bytes 524288 | tf_op jit(solution)/shard_map/psum | solution.py:21
  55.1 525.6 %copy-start.1 = (f32[512,256]{1,0:T(8,128)S(1)}, f32[512,256]{1,0:T(8,128)}, u32[]{:S(2)}) copy-start(f32[512,256]{1,0:T(8,128)} %reduce-scatter.2.cloned.1.call-done) | copy-start | bytes 1572868
  559.6 0.7 copy-start.2
Sparse Core Ops, SparseCore 0:
  11.9 40.2 reduce-scatter.1
  59.1 458.1 all-reduce.2
where the time goes:
time: 593 us
  waiting for transfers between devices  502 us (85%)
  other arithmetic  55.5 us (9%)
  between operations  15.5 us (3%)
  matrix products  10.5 us (2%)
  local copies, waits for them, and re-layouts  8.27 us (1%)
    psum x1, waiting for transfers between devices, shards(): gram = lax.psum(gram, ('space', 'tm'))  462 us
    reduce_scatter x1, waiting for transfers between devices, shards(): lax.psum_scatter(jnp.dot(snapshots, sketch, preferred_element_type=jnp.fl...  40.3 us
    another operation x6, other arithmetic, shards(): lower = jnp.linalg.cholesky(gram)  34 us
    another operation x2, other arithmetic, shards(): lax.linalg.triangular_solve(lower, sketched, left_side=False, lower=True,...  20.5 us
  transfers between devices with their start and end apart: 2, of which 2 were waited for; matrix products, arithmetic and copies ran while one was open for 0% of the time, Pallas kernels for 0%

commit v1 on v0

--- a/solution.py
+++ b/solution.py
@@ -18,7 +18,7 @@
         precision=lax.Precision.HIGHEST,
         preferred_element_type=jnp.float32,
     )
-    gram = lax.psum(gram, ("space", "tm"))
+    gram = lax.psum(lax.psum(gram, "space"), "tm")
     lower = jnp.linalg.cholesky(gram)
     orthonormal = lax.linalg.triangular_solve(
         lower, sketched, left_side=False, lower=True, transpose_a=True

time: 593 us -> 518 us (0.87)
  the two profiles are of different devices: /device:TPU:4 before, /device:TPU:8 now
where the time goes in v1:
time: 518 us
  waiting for transfers between devices  428 us (83%)
  other arithmetic  55.5 us (11%)
  between operations  15.2 us (3%)
  matrix products  10.5 us (2%)
  local copies, waits for them, and re-layouts  8.27 us (2%)
    psum x2, waiting for transfers between devices, shards(): gram = lax.psum(lax.psum(gram, 'space'), 'tm')  386 us
    reduce_scatter x1, waiting for transfers between devices, shards(): lax.psum_scatter(jnp.dot(snapshots, sketch, preferred_element_type=jnp.fl...  41.8 us
    another operation x6, other arithmetic, shards(): lower = jnp.linalg.cholesky(gram)  34 us
    another operation x2, other arithmetic, shards(): lax.linalg.triangular_solve(lower, sketched, left_side=False, lower=True,...  20.5 us
  transfers between devices with their start and end apart: 3, of which 3 were waited for; matrix products, arithmetic and copies ran while one was open for 0% of the time, Pallas kernels for 0%

profile of v1, /device:TPU:8, one launch (start us, length us, event | category | flops | bytes accessed | tf_op | source)
XLA Modules:
  0.0 517.6 jit_solution(1128079094507511957)
XLA Ops:
  7.2 0.0 copy-start
  7.2 0.0 reduce-scatter.2.cloned.1.call-start
  7.2 1.5 copy-done
  8.8 3.0 fusion.14
  11.8 0.0 reduce-scatter.2.cloned.1.call-update
  11.8 0.0 all-reduce.4.cloned.1.call-start
  11.8 41.8 %reduce-scatter.2.cloned.1.call-done = f32[512,256]{1,0:T(8,128)} async-done(((f32[2048,256]{1,0:T(8,128)}), f32[512,256]{1,0:T(8,128)}) %reduce-scatter.2.cloned.1.call-update) | async-done | bytes 524304 | tf_op jit(solution)/shard_map/reduce_scatter | solution.py:8
  53.6 2.9 fusion.15
  56.5 0.0 all-reduce.4.cloned.1.call-update
  56.6 0.0 all-reduce.6.cloned.1.call-start
  56.6 329.5 %all-reduce.4.cloned.1.call-done = f32[256,256]{0,1:T(8,128)} async-done(((f32[256,256]{0,1:T(8,128)}), f32[256,256]{0,1:T(8,128)}) %all-reduce.4.cloned.1.call-update) | async-done | bytes 262160 | tf_op jit(solution)/shard_map/psum | solution.py:21
  386.1 0.0 all-reduce.6.cloned.1.call-update
  386.2 0.0 copy-start.1
  386.2 56.4 %all-reduce.6.cloned.1.call-done = f32[256,256]{0,1:T(8,128)} async-done(((f32[256,256]{0,1:T(8,128)}), f32[256,256]{0,1:T(8,128)}) %all-reduce.6.cloned.1.call-update) | async-done | bytes 262160 | tf_op jit(solution)/shard_map/psum | solution.py:21
  442.6 1.1 copy.6
  443.7 1.0 fusion.5
  444.7 11.7 %cholesky.50 = f32[128,128]{1,0:T(8,128)S(1)} custom-call(f32[128,128]{1,0:T(8,128)S(1)} %cholesky.118), custom_call_target="Cholesky" | custom-call | tf_op jit(solution)/shard_map/jit(cholesky)/cholesky | solution.py:22
  456.4 9.8 %custom-call.14 = f32[1,128,128]{1,2,0:T(8,128)S(1)} custom-call(f32[1,128,128]{2,1,0:T(8,128)S(1)} %get-tuple-element.27), custom_call_target="InvertDiagBlocksLowerTriangular" | custom-call | tf_op jit(solution)/shard_map/jit(cholesky)/cholesky | solution.py:22
  466.3 0.2 constant_dynamic-update-slice_fusion.1
  466.5 0.3 convolution_subtract_fusion.1
  466.8 11.7 %cholesky.105 = f32[128,128]{1,0:T(8,128)S(1)} custom-call(f32[128,128]{1,0:T(8,128)S(1)} %convolution_subtract_fusion.1), custom_call_target="Cholesky" | custom-call | tf_op jit(solution)/shard_map/jit(cholesky)/cholesky | solution.py:22
  478.5 0.7 compare_reduce_fusion
  480.6 0.1 triangular_solve.58
  480.7 4.2 while.1
  480.9 0.6 fusion.26
  481.4 1.4 bitcast_dynamic-update-slice_fusion.2
  482.9 0.6 fusion.26
  483.5 1.4 bitcast_dynamic-update-slice_fusion.2
  484.9 0.0 copy-start.2
  485.0 0.6 copy-done.2
  485.6 20.5 %custom-call.15 = f32[2,128,128]{1,2,0:T(8,128)S(1)} custom-call(f32[2,128,128]{2,1,0:T(8,128)} %copy-done.2), custom_call_target="InvertDiagBlocksLowerTriangular" | custom-call | tf_op jit(solution)/shard_map/triangular_solve | solution.py:23
  506.1 0.0 copy-done.1
  506.1 0.4 fusion.3
  506.5 0.6 convolution_subtract_fusion
  507.1 0.4 fusion.7
  507.5 0.8 copy.7
  508.4 2.7 convolution_multiply_fusion
  (9 shorter events, 0.2 us)
Async XLA Ops:
  7.2 1.6 copy-start
  7.2 46.5 %reduce-scatter.2.cloned.1.call-start = ((), (), s32[]{:S(2)}) async-start(), calls=%async_computation.1 | async-start | bytes 2621440 | tf_op jit(solution)/shard_map/reduce_scatter | solution.py:8
  11.8 374.3 %all-reduce.4.cloned.1.call-start = ((), (), s32[]{:S(2)}) async-start(), calls=%async_computation.2 | async-start | bytes 524288 | tf_op jit(solution)/shard_map/psum | solution.py:21
  56.6 386.0 %all-reduce.6.cloned.1.call-start = ((), (), s32[]{:S(2)}) async-start(), calls=%async_computation.3 | async-start | bytes 524288 | tf_op jit(solution)/shard_map/psum | solution.py:21
  386.2 119.9 %copy-start.1 = (f32[512,256]{1,0:T(8,128)S(1)}, f32[512,256]{1,0:T(8,128)}, u32[]{:S(2)}) copy-start(f32[512,256]{1,0:T(8,128)} %reduce-scatter.2.cloned.1.call-done) | copy-start | bytes 1572868
  484.9 0.7 copy-start.2
Sparse Core Ops, SparseCore 0:
  11.9 41.6 reduce-scatter.1
  58.1 328.0 all-reduce.3
  388.6 54.0 all-reduce.5
